TPU v7x, 128 devices: a whole 4x4x4 slice. The times are simulated.
128 devices in a mesh: tile: 32 (over z, y, x_hi), lev: 4 (over x_lo, core).
Axes of the slice: x: 4 (x_hi: 2, x_lo: 2; x = x_hi * 2 + x_lo), y: 4, z: 4, core: 2. Of those that a mesh axis runs over, the one named last changes fastest.
Arguments:
- thermal_state: float32 [128, 131072], P('lev', 'tile'), may hold values from 0.5 to 1.5
- humidity_loading: float32 [128, 131072], P('lev', 'tile'), may hold values from 0 to 1
- interface_mixing_strength: float32 [128, 131072], P('lev', 'tile'), may hold values from 1 to 30
- passive_species: bfloat16 [8, 128, 131072], P(None, 'lev', 'tile'), may hold values from -6 to 6
- terrain_height: float32 [131072], P('tile'), may hold values from -6 to 6
- log_bottom_stress: float32 [131072], P('tile'), may hold values from -3 to 3
- side_length_share: float32 [6, 131072], P(None, 'tile'), may hold values from 0.5 to 2
- adjacency_table: int32 [6, 131072], P(None, 'tile'), may hold values from 0 to 6143, as said below
Outputs:
- gravity_height: float32 [128, 131072], P('lev', 'tile')
- force_divergence: float32 [128, 131072], P('lev', 'tile')
- new_tracers: float32 [8, 128, 131072], P(None, 'lev', 'tile')
Inputs may be any that keep to these rules, and one draw needn't show every extreme that they name: adjacency_table[m, c] is the position of column c's m-th neighbour among its tile's columns extended by 1024 columns of each adjacent tile on both sides (the band closes on itself); it lies within 1024 positions of the column's own position and is never the column itself.
All inputs are finite; a program needn't handle non-finite values.
Results may differ from a plain program's by a relative error of at most 0.00045.
Values may be sent and summed in bfloat16 or wider, within the bound.
A program may use at most 128 MiB of HBM per device.

v0:
```python
import jax
import jax.numpy as jnp
from jax import lax
from jax.sharding import PartitionSpec as P

HALO = 1024


humidity_multiplier = 0.608
mixing_rate = 0.05


def extended(cells, sides, width):
    for axis, dim in sides:
        count = lax.axis_size(axis)
        head = lax.slice_in_dim(cells, 0, width, axis=dim)
        tail = lax.slice_in_dim(cells, cells.shape[dim] - width, cells.shape[dim], axis=dim)
        cells = jnp.concatenate(
            [
                lax.ppermute(tail, axis, [(i, (i + 1) % count) for i in range(count)]),
                cells,
                lax.ppermute(head, axis, [((i + 1) % count, i) for i in range(count)]),
            ],
            axis=dim,
        )
    return cells


def shift_down(values, stride, filler):
    filler_block = jnp.full(values.shape[:-2] + (stride, values.shape[-1]), filler, values.dtype)
    return jnp.concatenate([filler_block, values[..., :-stride, :]], axis=-2)


def shift_up(values, stride, filler):
    filler_block = jnp.full(values.shape[:-2] + (stride, values.shape[-1]), filler, values.dtype)
    return jnp.concatenate([values[..., stride:, :], filler_block], axis=-2)


def cyclic_reduce(sub_diagonal, diagonal, super_diagonal, right_side):
    level_count = diagonal.shape[0]
    stride = 1
    while stride < level_count:
        left_factor = -sub_diagonal / shift_down(diagonal, stride, 1.0)
        right_factor = -super_diagonal / shift_up(diagonal, stride, 1.0)
        new_diagonal = (
            diagonal
            + left_factor * shift_down(super_diagonal, stride, 0.0)
            + right_factor * shift_up(sub_diagonal, stride, 0.0)
        )
        new_right = (
            right_side
            + left_factor * shift_down(right_side, stride, 0.0)
            + right_factor * shift_up(right_side, stride, 0.0)
        )
        sub_diagonal = left_factor * shift_down(sub_diagonal, stride, 0.0)
        super_diagonal = right_factor * shift_up(super_diagonal, stride, 0.0)
        diagonal = new_diagonal
        right_side = new_right
        stride = stride * 2
    return right_side / diagonal


def local(
    thermal_state,
    humidity_loading,
    interface_mixing_strength,
    passive_species,
    terrain_height,
    log_bottom_stress,
    side_length_share,
    adjacency_table,
):
    layers_in_piece, vertical_indices = thermal_state.shape
    level_total = layers_in_piece * lax.axis_size("lev")
    lev_index = lax.axis_index("lev")
    layer_indices = lev_index * layers_in_piece + lax.iota(jnp.int32, layers_in_piece)
    tracer_ext = extended(passive_species, (("tile", 2),), HALO)
    density_thermal = thermal_state * (1.0 + humidity_multiplier * humidity_loading)
    pieces = (
        lax.all_gather(thermal_state.astype(jnp.bfloat16), "lev", axis=0, tiled=True).astype(
            jnp.float32
        ),
        lax.all_gather(humidity_loading.astype(jnp.bfloat16), "lev", axis=0, tiled=True).astype(
            jnp.float32
        ),
    )
    piece_count = pieces[0].shape[0]
    add_source_ids = lax.iota(jnp.int32, piece_count)
    above_mask = add_source_ids[None, :] > layer_indices[:, None]
    same_mask = add_source_ids[None, :] == layer_indices[:, None]
    weights = (
        jnp.where(above_mask, 1.0, jnp.where(same_mask, 0.5, 0.0)).astype(jnp.float32) / level_total
    )
    piece_virtual = pieces[0] * (1.0 + humidity_multiplier * pieces[1])
    column_part = jnp.dot(
        weights, piece_virtual, precision=lax.Precision.HIGHEST, preferred_element_type=jnp.float32
    )
    gravity_height = terrain_height[None, :] + column_part
    stacked = jnp.concatenate([gravity_height, log_bottom_stress[None, :]], axis=0)
    stacked_ext = extended(stacked, (("tile", 1),), HALO)
    tracer_count = passive_species.shape[0]
    tracer_rows = tracer_ext.reshape(tracer_count * layers_in_piece, tracer_ext.shape[2])
    own_tracers = passive_species.reshape(tracer_count * layers_in_piece, vertical_indices).astype(
        jnp.float32
    )
    share_total = jnp.sum(side_length_share, axis=0)
    block_width = min(512, vertical_indices)
    block_count = vertical_indices // block_width
    window_width = block_width + 2 * HALO
    source_ids = lax.iota(jnp.int32, window_width)

    def stencil_block(block_number, outputs):
        force_out, laplace_out = outputs
        start = block_number * block_width
        local_targets = lax.dynamic_slice_in_dim(adjacency_table, start, block_width, 1) - start
        local_shares = lax.dynamic_slice_in_dim(side_length_share, start, block_width, 1)
        hits = source_ids[None, :, None] == local_targets[:, None, :]
        weighting = jnp.sum(jnp.where(hits, local_shares[:, None, :], 0.0), axis=0)
        stack_window = lax.dynamic_slice_in_dim(stacked_ext, start, window_width, 1)
        tracer_window = lax.dynamic_slice_in_dim(tracer_rows, start, window_width, 1).astype(
            jnp.float32
        )
        near_stack = jnp.dot(
            stack_window,
            weighting,
            precision=lax.Precision.HIGHEST,
            preferred_element_type=jnp.float32,
        )
        near_tracer = jnp.dot(
            tracer_window,
            weighting,
            precision=lax.Precision.HIGHEST,
            preferred_element_type=jnp.float32,
        )
        own_stack = lax.dynamic_slice_in_dim(stacked, start, block_width, 1)
        own_virtual = lax.dynamic_slice_in_dim(density_thermal, start, block_width, 1)
        own_tracer = lax.dynamic_slice_in_dim(own_tracers, start, block_width, 1)
        own_total = lax.dynamic_slice_in_dim(share_total, start, block_width, 0)
        height_part = near_stack[:-1] - own_stack[:-1] * own_total[None, :]
        stress_part = near_stack[-1] - own_stack[-1] * own_total
        force_block = height_part + own_virtual * stress_part[None, :]
        laplace_block = near_tracer - own_tracer * own_total[None, :]
        force_out = lax.dynamic_update_slice_in_dim(force_out, force_block, start, 1)
        laplace_out = lax.dynamic_update_slice_in_dim(laplace_out, laplace_block, start, 1)
        return (force_out, laplace_out)

    force_divergence, laplace = lax.fori_loop(
        0, block_count, stencil_block, (jnp.zeros_like(gravity_height), jnp.zeros_like(own_tracers))
    )
    mixed = (own_tracers + mixing_rate * laplace).reshape(
        tracer_count, layers_in_piece, vertical_indices
    )
    gas_constant_share = jnp.where(
        layer_indices[:, None] == 0, 0.0, interface_mixing_strength * density_thermal
    )
    packed = jnp.concatenate([mixed, gas_constant_share[None]], axis=0)
    column_data = lax.all_to_all(packed, "lev", split_axis=2, concat_axis=1, tiled=True)
    column_mixed = column_data[:-1]
    column_kappa = column_data[-1]
    below_kappa = jnp.concatenate(
        [column_kappa[1:], jnp.zeros((1, column_kappa.shape[1]), jnp.float32)], axis=0
    )
    solved = cyclic_reduce(
        -column_kappa, 1.0 + column_kappa + below_kappa, -below_kappa, column_mixed
    )
    new_tracers = lax.all_to_all(solved, "lev", split_axis=1, concat_axis=2, tiled=True)
    return (gravity_height, force_divergence, new_tracers)


def solution(mesh):
    return jax.shard_map(
        local,
        mesh=mesh,
        in_specs=(
            P("lev", "tile"),
            P("lev", "tile"),
            P("lev", "tile"),
            P(None, "lev", "tile"),
            P("tile"),
            P("tile"),
            P(None, "tile"),
            P(None, "tile"),
        ),
        out_specs=(P("lev", "tile"), P("lev", "tile"), P(None, "lev", "tile")),
        check_vma=False,
    )
```

profile of v0, /device:TPU:1, one launch (start us, length us, event | category | flops | bytes accessed | tf_op | source)
XLA Modules:
  0.0 563.7 jit_solution(516044548046280661)
XLA Ops:
  12.5 9.5 %collective-permute-start.3 = (bf16[8,32,1024]{2,1,0:T(8,128)(2,1)}, bf16[8,32,1024]{2,1,0:T(8,128)(2,1)S(1)}, u32[]{:S(2)}, u32[]{:S(2)}) collective-permute-start(bf16[8,32,1024]{2,1,0:T(8,128)(2,1)} %get-tuple-element.308), channel_id=1, source_target_pairs={{4,0},{8,4},{12,8},{16,12},{20,16},{24,20},{28,24},{32,28},{36,32}... | collective-permute-start | bytes 1572872 | tf_op jit(solution)/shard_map/ppermute | solution.py:22
  24.7 16.6 %collective-permute-done.3 = bf16[8,32,1024]{2,1,0:T(8,128)(2,1)S(1)} collective-permute-done((bf16[8,32,1024]{2,1,0:T(8,128)(2,1)}, bf16[8,32,1024]{2,1,0:T(8,128)(2,1)S(1)}, u32[]{:S(2)}, u32[]{:S(2)}) %collective-permute-start.3) | collective-permute-done | bytes 524320 | tf_op jit(solution)/shard_map/ppermute | solution.py:22
  42.1 11.4 %collective-permute-done.2 = bf16[8,32,1024]{2,1,0:T(8,128)(2,1)} collective-permute-done((bf16[8,32,1024]{2,1,0:T(8,128)(2,1)S(1)}, bf16[8,32,1024]{2,1,0:T(8,128)(2,1)}, u32[]{:S(2)}, u32[]{:S(2)}) %collective-permute-start.2) | collective-permute-done | bytes 524320 | tf_op jit(solution)/shard_map/ppermute | solution.py:20
  55.6 11.7 %all-gather.3.cloned.1.call-done = bf16[128,4096]{1,0:T(8,128)(2,1)} async-done(((bf16[32,4096]{1,0:T(8,128)(2,1)}), bf16[128,4096]{1,0:T(8,128)(2,1)}) %all-gather.3.cloned.1.call-update) | async-done | bytes 1048592 | tf_op jit(solution)/shard_map/all_gather | solution.py:80
  70.4 7.0 %collective-permute-start.1 = (f32[33,1024]{1,0:T(8,128)S(1)}, f32[33,1024]{1,0:T(8,128)S(1)}, u32[]{:S(2)}, u32[]{:S(2)}) collective-permute-start(f32[33,1024]{1,0:T(8,128)S(1)} %get-tuple-element.310), channel_id=1, source_target_pairs={{4,0},{8,4},{12,8},{16,12},{20,16},{24,20},{28,24},{32,28},{36,32}... | collective-permute-start | bytes 405512 | tf_op jit(solution)/shard_map/ppermute | solution.py:22
  81.2 7.8 %collective-permute-done = f32[33,1024]{1,0:T(8,128)S(1)} collective-permute-done((f32[33,1024]{1,0:T(8,128)S(1)}, f32[33,1024]{1,0:T(8,128)S(1)}, u32[]{:S(2)}, u32[]{:S(2)}) %collective-permute-start) | collective-permute-done | bytes 135200 | tf_op jit(solution)/shard_map/ppermute | solution.py:20
  93.3 173.1 %while.16 = (s32[]{:T(128)}, f32[32,4096]{1,0:T(8,128)}, f32[256,4096]{1,0:T(8,128)}, f32[33,6144]{1,0:T(8,128)}, s32[6,4096]{1,0:T(8,128)}, /*index=5*/f32[6,40...) while((s32[]{:T(128)}, f32[32,4096]{1,0:T(8,128)}, ...), condition=%wide.region_3.4_spmd.clone, body=%wide.region_1.3_spmd.clone.sunk | while | flops 4568190976 | bytes 18925852 | solution.py:147
  94.1 6.8 %select_reduce_fusion.2 = f32[2560,512]{1,0:T(8,128)} fusion(f32[6,512]{1,0:T(8,128)S(1)} %constant_dynamic-slice_fusion.2, s32[6,512]{1,0:T(8,128)S(1)} %dynamic-slice_subtract_fusion.2), kind=kLoop, calls=%fused_computation.2.clone.1 | loop fusion | flops 22282240 | bytes 5267456 | tf_op jit(solution)/shard_map/while/body/eval_jaxpr/reduce_sum | solution.py:118
  115.7 6.8 %select_reduce_fusion.2 = f32[2560,512]{1,0:T(8,128)} fusion(f32[6,512]{1,0:T(8,128)S(1)} %constant_dynamic-slice_fusion.2, s32[6,512]{1,0:T(8,128)S(1)} %dynamic-slice_subtract_fusion.2), kind=kLoop, calls=%fused_computation.2.clone.1 | loop fusion | flops 22282240 | bytes 5267456 | tf_op jit(solution)/shard_map/while/body/eval_jaxpr/reduce_sum | solution.py:118
  130.6 6.0 %fusion.80 = f32[256,4096]{1,0:T(8,128)} fusion(f32[256,4096]{1,0:T(8,128)} %get-tuple-element.445, s32[]{:T(128)S(6)} %select_n.62, f32[2560,512]{1,0:T(8,128)} %select_reduce_fusion.2, bf16[256,6144]{1,0:T(8,128)(2,1)S(1)} %get-tuple-element.469, s32[]{:T(128)S(6)} %select_n.63, f32[256,4096]{1,0:T(8,128)} %get-tuple-element.470, ...), kind=kOutput, calls=%fused_computation.6.clone.1 | convolution fusion | flops 4026793984 | bytes 7604232 | tf_op jit(solution)/shard_map/while/body/eval_jaxpr/dot_general | solution.py:129
  137.3 6.8 %select_reduce_fusion.2 = f32[2560,512]{1,0:T(8,128)} fusion(f32[6,512]{1,0:T(8,128)S(1)} %constant_dynamic-slice_fusion.2, s32[6,512]{1,0:T(8,128)S(1)} %dynamic-slice_subtract_fusion.2), kind=kLoop, calls=%fused_computation.2.clone.1 | loop fusion | flops 22282240 | bytes 5267456 | tf_op jit(solution)/shard_map/while/body/eval_jaxpr/reduce_sum | solution.py:118
  159.0 6.8 %select_reduce_fusion.2 = f32[2560,512]{1,0:T(8,128)} fusion(f32[6,512]{1,0:T(8,128)S(1)} %constant_dynamic-slice_fusion.2, s32[6,512]{1,0:T(8,128)S(1)} %dynamic-slice_subtract_fusion.2), kind=kLoop, calls=%fused_computation.2.clone.1 | loop fusion | flops 22282240 | bytes 5267456 | tf_op jit(solution)/shard_map/while/body/eval_jaxpr/reduce_sum | solution.py:118
  180.6 6.8 %select_reduce_fusion.2 = f32[2560,512]{1,0:T(8,128)} fusion(f32[6,512]{1,0:T(8,128)S(1)} %constant_dynamic-slice_fusion.2, s32[6,512]{1,0:T(8,128)S(1)} %dynamic-slice_subtract_fusion.2), kind=kLoop, calls=%fused_computation.2.clone.1 | loop fusion | flops 22282240 | bytes 5267456 | tf_op jit(solution)/shard_map/while/body/eval_jaxpr/reduce_sum | solution.py:118
  202.2 6.8 %select_reduce_fusion.2 = f32[2560,512]{1,0:T(8,128)} fusion(f32[6,512]{1,0:T(8,128)S(1)} %constant_dynamic-slice_fusion.2, s32[6,512]{1,0:T(8,128)S(1)} %dynamic-slice_subtract_fusion.2), kind=kLoop, calls=%fused_computation.2.clone.1 | loop fusion | flops 22282240 | bytes 5267456 | tf_op jit(solution)/shard_map/while/body/eval_jaxpr/reduce_sum | solution.py:118
  223.9 6.8 %select_reduce_fusion.2 = f32[2560,512]{1,0:T(8,128)} fusion(f32[6,512]{1,0:T(8,128)S(1)} %constant_dynamic-slice_fusion.2, s32[6,512]{1,0:T(8,128)S(1)} %dynamic-slice_subtract_fusion.2), kind=kLoop, calls=%fused_computation.2.clone.1 | loop fusion | flops 22282240 | bytes 5267456 | tf_op jit(solution)/shard_map/while/body/eval_jaxpr/reduce_sum | solution.py:118
  245.5 6.8 %select_reduce_fusion.2 = f32[2560,512]{1,0:T(8,128)} fusion(f32[6,512]{1,0:T(8,128)S(1)} %constant_dynamic-slice_fusion.2, s32[6,512]{1,0:T(8,128)S(1)} %dynamic-slice_subtract_fusion.2), kind=kLoop, calls=%fused_computation.2.clone.1 | loop fusion | flops 22282240 | bytes 5267456 | tf_op jit(solution)/shard_map/while/body/eval_jaxpr/reduce_sum | solution.py:118
  272.6 22.1 %copy.33 = f32[9,32,4096]{1,0,2:T(8,128)} copy(f32[9,32,4096]{2,1,0:T(8,128)} %pad_maximum_fusion) | data formatting | bytes 9437184 | tf_op jit(solution)/shard_map/concatenate | solution.py:156
  294.7 28.4 %reshape.50 = f32[4,1,294912]{2,1,0:T(1,128)} reshape(f32[4096,9,32]{2,1,0:T(8,128)} %bitcast.36) | data formatting | bytes 9437184
  323.1 59.7 %all_to_all.33 = f32[4,1,294912]{2,1,0:T(1,128)} all-to-all(f32[4,1,294912]{2,1,0:T(1,128)} %reshape.50), channel_id=1, replica_groups=mesh['tile'=32,'lev'=4] {'lev'}, dimensions={0} | all-to-all | bytes 9437184 | tf_op jit(solution)/shard_map/all_to_all | solution.py:157
  383.3 16.9 %reduce = f32[4,294912]{1,0:T(4,128)} reduce(f32[4,1,294912]{2,1,0:T(1,128)} %all_to_all.33, f32[]{:T(128)} %broadcast.165), dimensions={1}, to_apply=%all_to_all.24.reduce_sub_computation | reduce | bytes 9437188 | tf_op jit(solution)/shard_map/all_to_all | solution.py:157
  400.2 24.9 %reshape.51 = f32[4096,9,32]{2,1,0:T(8,128)} reshape(f32[4,294912]{1,0:T(4,128)} %reduce) | data formatting | bytes 9437184
  425.1 21.3 %copy.40 = f32[9,32,4,1024]{3,2,1,0:T(4,128)} copy(f32[9,32,4,1024]{1,0,3,2:T(8,128)} %bitcast.37) | data formatting | bytes 9437184 | tf_op jit(solution)/shard_map/all_to_all | solution.py:157
  495.2 50.7 %all_to_all.34 = f32[8,128,1024]{2,0,1:T(8,128)S(1)} all-to-all(f32[8,128,1024]{2,0,1:T(8,128)S(1)} %copy.37), channel_id=1, replica_groups=mesh['tile'=32,'lev'=4] {'lev'}, dimensions={1} | all-to-all | bytes 8388608 | tf_op jit(solution)/shard_map/all_to_all | solution.py:166
  550.5 6.0 %all_to_all.30 = f32[8,32,4096]{2,1,0:T(8,128)} reshape(f32[8,32,4,1024]{3,2,1,0:T(4,128)} %copy.39) | data formatting | bytes 8388608 | tf_op jit(solution)/shard_map/all_to_all | solution.py:166
  (186 shorter events, 194.1 us)
Async XLA Ops:
  7.2 14.8 %copy-start = (bf16[8,32,4096]{2,1,0:T(8,128)(2,1)S(1)}, bf16[8,32,4096]{2,1,0:T(8,128)(2,1)}, u32[]{:S(2)}) copy-start(bf16[8,32,4096]{2,1,0:T(8,128)(2,1)} %param.13) | copy-start | bytes 6291460
  7.2 48.4 %all-gather.5.cloned.1.call-start = ((), (), s32[]{:S(2)}) async-start(), calls=%async_computation.3 | async-start | bytes 1310720 | tf_op jit(solution)/shard_map/all_gather | solution.py:83
  10.3 14.3 %copy-start.16 = (f32[6,4096]{1,0:T(8,128)S(1)}, f32[6,4096]{1,0:T(8,128)}, u32[]{:S(2)}) copy-start(f32[6,4096]{1,0:T(8,128)} %param.16) | copy-start | bytes 294916
  10.3 56.9 %all-gather.3.cloned.1.call-start = ((), (), s32[]{:S(2)}) async-start(), calls=%async_computation.2 | async-start | bytes 1310720 | tf_op jit(solution)/shard_map/all_gather | solution.py:80
  12.5 28.9 %collective-permute-start.3 = (bf16[8,32,1024]{2,1,0:T(8,128)(2,1)}, bf16[8,32,1024]{2,1,0:T(8,128)(2,1)S(1)}, u32[]{:S(2)}, u32[]{:S(2)}) collective-permute-start(bf16[8,32,1024]{2,1,0:T(8,128)(2,1)} %get-tuple-element.308), channel_id=1, source_target_pairs={{4,0},{8,4},{12,8},{16,12},{20,16},{24,20},{28,24},{32,28},{36,32}... | collective-permute-start | bytes 1572872 | tf_op jit(solution)/shard_map/ppermute | solution.py:22
  22.0 31.5 %collective-permute-start.2 = (bf16[8,32,1024]{2,1,0:T(8,128)(2,1)S(1)}, bf16[8,32,1024]{2,1,0:T(8,128)(2,1)}, u32[]{:S(2)}, u32[]{:S(2)}) collective-permute-start(bf16[8,32,1024]{2,1,0:T(8,128)(2,1)S(1)} %get-tuple-element.307), channel_id=1, source_target_pairs={{0,4},{4,8},{8,12},{12,16},{16,20},{20,24},{24,28},{28,32},{32,36}... | collective-permute-start | bytes 1572872 | tf_op jit(solution)/shard_map/ppermute | solution.py:20
  24.7 42.6 %copy-start.18 = (f32[4096]{0:T(1024)S(1)}, f32[4096]{0:T(1024)}, u32[]{:S(2)}) copy-start(f32[4096]{0:T(1024)} %param.14) | copy-start | bytes 49156
  24.7 45.6 %copy-start.17 = (f32[4096]{0:T(1024)S(1)}, f32[4096]{0:T(1024)}, u32[]{:S(2)}) copy-start(f32[4096]{0:T(1024)} %param.15) | copy-start | bytes 49156
  70.3 18.6 %copy-start.1 = (f32[32,4096]{1,0:T(8,128)}, f32[32,4096]{1,0:T(8,128)S(1)}, u32[]{:S(2)}) copy-start(f32[32,4096]{1,0:T(8,128)S(1)} %convolution_add_fusion) | copy-start | bytes 1572868
  70.4 10.8 %collective-permute-start.1 = (f32[33,1024]{1,0:T(8,128)S(1)}, f32[33,1024]{1,0:T(8,128)S(1)}, u32[]{:S(2)}, u32[]{:S(2)}) collective-permute-start(f32[33,1024]{1,0:T(8,128)S(1)} %get-tuple-element.310), channel_id=1, source_target_pairs={{4,0},{8,4},{12,8},{16,12},{20,16},{24,20},{28,24},{32,28},{36,32}... | collective-permute-start | bytes 405512 | tf_op jit(solution)/shard_map/ppermute | solution.py:22
  77.4 11.5 %collective-permute-start = (f32[33,1024]{1,0:T(8,128)S(1)}, f32[33,1024]{1,0:T(8,128)S(1)}, u32[]{:S(2)}, u32[]{:S(2)}) collective-permute-start(f32[33,1024]{1,0:T(8,128)S(1)} %get-tuple-element.309), channel_id=1, source_target_pairs={{0,4},{4,8},{8,12},{12,16},{16,20},{20,24},{24,28},{28,32},{32,36}... | collective-permute-start | bytes 405512 | tf_op jit(solution)/shard_map/ppermute | solution.py:20
  266.4 3.5 copy-start.6
  456.8 3.7 copy-start.2
  460.5 2.2 copy-start.3
  460.5 2.2 copy-start.7
  460.5 2.2 copy-start.12
  469.2 2.2 copy-start.4
  469.3 2.2 copy-start.8
  469.3 2.2 copy-start.10
  477.2 2.2 copy-start.5
  477.2 2.2 copy-start.9
  477.2 2.2 copy-start.11
  482.1 2.1 copy-start.13
  486.5 1.2 copy-start.14
  (1 other events, 0.8 us)
Sparse Core Ops, SparseCore 0:
  10.5 33.0 all-gather.4
  45.7 21.4 all-gather.2
where the time goes:
time: 570 us; the launch traced here: 564 us
  local copies, waits for them, and re-layouts  145 us (25%)
  other arithmetic  129 us (23%)
  blocking collectives  110 us (19%)
  matrix products  97 us (17%)
  waiting for transfers between devices  50.2 us (9%)
  starting transfers between devices  16.8 us (3%)
  between operations  14.9 us (3%)
    all_to_all x1, blocking collectives, local(): lax.all_to_all(packed, 'lev', split_axis=2, concat_axis=1, tiled=True)  59.7 us
    reduce_sum x8, other arithmetic, stencil_block(): weighting = jnp.sum(jnp.where(hits, local_shares[:, None, :], 0.0), axis=0)  54.6 us
    unnamed x40, local copies, waits for them, and re-layouts  54.2 us
    all_to_all x1, blocking collectives, local(): lax.all_to_all(solved, 'lev', split_axis=1, concat_axis=2, tiled=True)  50.7 us
    dot_general x8, matrix products, stencil_block(): jnp.dot(tracer_window, weighting, precision=lax.Precision.HIGHEST, prefer...  47.9 us
    dot_general x8, matrix products, stencil_block(): jnp.dot(stack_window, weighting, precision=lax.Precision.HIGHEST, preferr...  46 us
    concatenate x1, local copies, waits for them, and re-layouts, local(): packed = jnp.concatenate([mixed, gas_constant_share[None]], axis=0)  22.1 us
    all_to_all x2, local copies, waits for them, and re-layouts, local(): lax.all_to_all(packed, 'lev', split_axis=2, concat_axis=1, tiled=True)  21.8 us
  transfers between devices with their start and end apart: 6, of which 5 were waited for; matrix products, arithmetic and copies ran while one was open for 1% of the time, Pallas kernels for 0%

commit v1 on v0

v1 whole, which is shorter than its diff:
```python
import jax
import jax.numpy as jnp
from jax import lax
from jax.experimental import pallas as pl
from jax.experimental.pallas import tpu as pltpu
from jax.sharding import PartitionSpec as P

BF = jnp.bfloat16
F32 = jnp.float32
MESH = pl.DeviceIdType.MESH
HALO = 1024
COLS = 4096
EXT = COLS + 2 * HALO
LEV = 32
NTR = 8
BLK = 256
WIN = BLK + 2 * HALO
NBLK = COLS // BLK
GRP = 512
ROWS = 336
TILES = 32
LEVELS = 128.0

R_SUM = 0
R_KAP = 3
R_TRC = 4
R_VIR = 20
R_BAS = 22
R_COF = 24
R_CHP = 25
R_YB = 26
R_YC = 29
N_REMOTE = 32

L_NAT = 0
L_FOLD = 2
L_TRC = 26
L_SMALL = 34
N_LOCAL = 38
L_OUT = 38
N_OUT = 51
SPANS = ((1024, 2048), (0, 1024), (3072, 1024))


def kernel(
    th_ref, hu_ref, mx_ref, tr_ref, te_ref, lo_ref, sh_ref, ad_ref,
    y_out, ends_out, g_out, h_out, gh_out, fo_out,
    xa, w, mm, fo, gh, vn, tn, hn, tf, hf, sf,
    rf, pf, ef, gf, hfo, sums, kbot, ktop, vb, vh, bl, blh,
    cfo, cfi, cho, chi, dq, yb, yp, yc, yo, xe, ter, los, shr, adj, shm, shi, slo, tot,
    ssem, rsem, lsem,
):
    tile = lax.axis_index("tile")
    lev = lax.axis_index("lev")
    core = lev % 2
    chip = lev // 2
    partner = chip * 2 + 1 - core
    across = (lev + 2) % 4
    diagonal = (partner + 2) % 4
    above = (lev + 3) % 4
    nxt = ((tile + 1) % TILES, lev)
    prv = ((tile + TILES - 1) % TILES, lev)
    peers = ((tile, partner), (tile, across), (tile, diagonal))

    bar = pltpu.get_barrier_semaphore()
    for q in peers + (nxt, prv):
        pl.semaphore_signal(bar, inc=1, device_id=q, device_id_type=MESH)

    def remote(i, src, dst, to):
        return pltpu.make_async_remote_copy(
            src_ref=src, dst_ref=dst, send_sem=ssem.at[i], recv_sem=rsem.at[i],
            device_id=to, device_id_type=MESH)

    nat = [pltpu.make_async_copy(s, d, lsem.at[L_NAT + i]) for i, (s, d) in enumerate(((th_ref, tn), (hu_ref, hn)))]
    small = [
        pltpu.make_async_copy(s, d, lsem.at[L_SMALL + i])
        for i, (s, d) in enumerate(((te_ref, ter), (lo_ref, los), (sh_ref, shr), (ad_ref, adj)))
    ]
    fold = []
    for i, (s, d) in enumerate(((th_ref, tf), (hu_ref, hf), (mx_ref, sf))):
        for g in range(8):
            fold.append(
                pltpu.make_async_copy(s.at[:, pl.ds(GRP * g, GRP)], d.at[:, g, :], lsem.at[L_FOLD + 8 * i + g])
            )
    trc = [
        pltpu.make_async_copy(tr_ref.at[n], xa.at[pl.ds(LEV * n, LEV), pl.ds(HALO, COLS)], lsem.at[L_TRC + n])
        for n in range(NTR)
    ]
    for c in nat + fold + small + trc:
        c.start()

    row = lax.broadcasted_iota(jnp.int32, (48, LEV), 0)
    col = lax.broadcasted_iota(jnp.int32, (48, LEV), 1)
    tri = jnp.where(row >= LEV, 1.0, jnp.where(col > row, 1.0, jnp.where(col == row, 0.5, 0.0))).astype(BF)
    for c in nat:
        c.wait()

    def natural(i, _):
        cs = pl.ds(pl.multiple_of(i * GRP, GRP), GRP)
        v = tn[:, cs] * (1.0 + 0.608 * hn[:, cs])
        vn[:, cs] = v
        v1 = v.astype(BF)
        vb[:, cs] = v1
        rest = v - v1.astype(F32)
        v2 = rest.astype(BF)
        v3 = (rest - v2.astype(F32)).astype(BF)
        part = jnp.dot(tri, v1, preferred_element_type=F32)
        part = part + jnp.dot(tri, v2, preferred_element_type=F32)
        part = part + jnp.dot(tri, v3, preferred_element_type=F32)
        gh[:, cs] = part[:LEV]
        sums[0, :, cs] = part[LEV : LEV + 1]
        return 0

    lax.fori_loop(0, 8, natural, 0)
    for c in fold:
        c.wait()
    for k in range(LEV):
        kap = sf[k] * (tf[k] * (1.0 + 0.608 * hf[k]))
        if k == 0:
            kap = jnp.where(lev == 0, 0.0, kap)
            ktop[...] = kap
        sf[k] = kap

    pl.semaphore_wait(bar, 5)
    c_sum = [remote(R_SUM + d, sums.at[0], sums.at[1 + d], peers[d]) for d in range(3)]
    c_kap = remote(R_KAP, ktop, kbot, (tile, above))
    for c in c_sum:
        c.start()
    c_kap.start()
    c_trc = []
    for n in range(NTR):
        rows = pl.ds(LEV * n, LEV)
        c_trc.append(remote(R_TRC + n, tr_ref.at[n, :, pl.ds(COLS - HALO, HALO)], xa.at[rows, pl.ds(0, HALO)], nxt))
        c_trc.append(
            remote(R_TRC + 8 + n, tr_ref.at[n, :, pl.ds(0, HALO)], xa.at[rows, pl.ds(HALO + COLS, HALO)], prv)
        )
    for c in c_trc:
        c.start()

    c_kap.wait_recv()
    e = None
    gg = None
    for k in range(LEV):
        a = sf[k]
        below = sf[k + 1] if k < LEV - 1 else kbot[...]
        d = 1.0 + a + below
        if k:
            d = d - a * e
        r = 1.0 / d
        p = a * r
        e = below * r
        gg = p * gg if k else p
        rf[k] = r
        pf[k] = p
        ef[k] = e
        gf[k] = gg
    hh = e
    hfo[LEV - 1] = hh
    cfo[1] = gg
    cfo[3] = hh
    for k in range(LEV - 2, -1, -1):
        e = ef[k]
        gg = gf[k] + e * gg
        hh = e * hh
        gf[k] = gg
        hfo[k] = hh
    cfo[0] = gg
    cfo[2] = hh
    c_cof = remote(R_COF, cfo, cfi, (tile, partner))
    c_cof.start()

    for c in small:
        c.wait()
    for c in c_sum:
        c.wait_recv()
    peer_levs = (partner, across, diagonal)

    def split(v):
        hi = v.astype(BF)
        return hi, (v - hi.astype(F32)).astype(BF)

    sub16 = lax.broadcasted_iota(jnp.int32, (16, GRP), 0)

    def put_extra(cs, height, stress):
        hi, low = split(height)
        xa[pl.ds(256, LEV), cs] = hi
        xa[pl.ds(304, LEV), cs] = low
        shi_, slo_ = split(stress)
        both = jnp.where(
            sub16 == 0,
            jnp.broadcast_to(shi_.astype(F32), (16, GRP)),
            jnp.where(sub16 == 1, jnp.broadcast_to(slo_.astype(F32), (16, GRP)), 0.0),
        )
        xa[pl.ds(288, 16), cs] = both.astype(BF)

    def heights(i, _):
        cs = pl.ds(pl.multiple_of(i * GRP, GRP), GRP)
        below = jnp.zeros((1, GRP), F32)
        for d in range(3):
            below = below + jnp.where(peer_levs[d] > lev, sums[1 + d, :, cs], 0.0)
        base = ter[:, cs] + below / LEVELS
        stress = los[:, cs]
        bl[pl.ds(0, 1), cs] = base
        bl[pl.ds(1, 1), cs] = stress
        height = base + gh[:, cs] / LEVELS
        gh[:, cs] = height
        put_extra(pl.ds(pl.multiple_of(HALO + i * GRP, GRP), GRP), height, stress)
        return 0

    lax.fori_loop(0, 8, heights, 0)
    c_hal = []
    for d, (lo, to) in enumerate(((COLS - HALO, nxt), (0, prv))):
        c_hal.append(remote(R_VIR + d, vb.at[:, pl.ds(lo, HALO)], vh.at[d], to))
        c_hal.append(remote(R_BAS + d, bl.at[:, pl.ds(lo, HALO)], blh.at[d], to))
    for c in c_hal:
        c.start()
    out_gh = pltpu.make_async_copy(gh, gh_out, lsem.at[L_OUT])
    out_gh.start()

    t = [adj[pl.ds(m, 1), :] for m in range(6)]
    s = [shr[pl.ds(m, 1), :] for m in range(6)]
    total = s[0]
    for m in range(1, 6):
        total = total + s[m]
    tot[...] = total
    for m in range(6):
        acc = s[m]
        for q in range(m):
            acc = acc + jnp.where(t[q] == t[m], s[q], 0.0)
        shm[pl.ds(m, 1), :] = acc
    merged = shm[...]
    high = merged.astype(BF)
    shi[...] = high
    slo[...] = (merged - high.astype(F32)).astype(BF)

    def weights(j, _):
        cs = pl.ds(pl.multiple_of(j * BLK, BLK), BLK)
        place = (adj[:, cs] - j * BLK).astype(F32)
        high = shi[:, cs]
        low = slo[:, cs]
        ids = lax.broadcasted_iota(jnp.int32, (BLK, BLK), 0).astype(F32).astype(BF)
        hs = [jnp.broadcast_to(high[m : m + 1], (BLK, BLK)) for m in range(6)]
        ls = [jnp.broadcast_to(low[m : m + 1], (BLK, BLK)) for m in range(6)]
        for r in range(9):
            u = jnp.clip(place - float(BLK * r), -1.0, float(BLK)).astype(BF)
            wh = jnp.zeros((BLK, BLK), BF)
            wl = jnp.zeros((BLK, BLK), BF)
            for m in range(6):
                hit = jnp.broadcast_to(u[m : m + 1], (BLK, BLK)) == ids
                wh = jnp.where(hit, hs[m], wh)
                wl = jnp.where(hit, ls[m], wl)
            w[j, 0, pl.ds(BLK * r, BLK), :] = wh
            w[j, 1, pl.ds(BLK * r, BLK), :] = wl
        return 0

    def product(j, lo, hi, rows, wide):
        n = BLK * (hi - lo)
        x = xa[rows, pl.ds(pl.multiple_of(BLK * (j + lo), BLK), n)]
        ws = pl.ds(BLK * lo, n)
        return jnp.dot(x, w[j, 0, ws, :], preferred_element_type=F32) + jnp.dot(
            x, w[j, 1, ws, :], preferred_element_type=F32
        )

    def own_part(j, lo, hi):
        cs = pl.ds(pl.multiple_of(j * BLK, BLK), BLK)
        es = pl.ds(pl.multiple_of(HALO + j * BLK, BLK), BLK)
        a = product(j, lo, hi, pl.ds(0, ROWS), True)
        total = tot[:, cs]
        own = xa[pl.ds(0, 256), es].astype(F32)
        mixed = own * (1.0 - 0.05 * total) + 0.05 * a[:256]
        mm[2 * j] = mixed[:, :128]
        mm[2 * j + 1] = mixed[:, 128:]
        stress = a[288:289] + a[289:290] - los[:, cs] * total
        fo[:, cs] = (a[256:288] + a[304:336] - gh[:, cs] * total) + vn[:, cs] * stress

    for c in trc:
        c.wait()
    lax.fori_loop(0, NBLK, weights, 0)

    def interior(i, _):
        own_part(4 + i, 0, 9)
        return 0

    lax.fori_loop(0, 8, interior, 0)

    def bc(ref, k, g):
        return jnp.broadcast_to(ref[k, pl.ds(g, 1), :], (NTR, GRP))

    def solve(g):
        def lane(ref, k, q):
            return jnp.broadcast_to(ref[k, pl.ds(g, 1), pl.ds(128 * q, 128)], (NTR, 128))

        def at(k):
            return pl.ds(k, NTR, stride=LEV)

        f = [None] * 4
        for k in range(LEV):
            for q in range(4):
                v = mm[4 * g + q, at(k), :] * lane(rf, k, q)
                f[q] = v + lane(pf, k, q) * f[q] if k else v
                mm[4 * g + q, at(k), :] = f[q]
        for q in range(4):
            yb[1, :, pl.ds(g * GRP + 128 * q, 128)] = f[q]
        for k in range(LEV - 2, -1, -1):
            for q in range(4):
                f[q] = mm[4 * g + q, at(k), :] + lane(ef, k, q) * f[q]
                mm[4 * g + q, at(k), :] = f[q]
        for q in range(4):
            yb[0, :, pl.ds(g * GRP + 128 * q, 128)] = f[q]

    def ends(i):
        cs = pl.ds(*SPANS[i])
        return remote(R_YB + i, yb.at[:, :, cs], yp.at[:, :, cs], (tile, partner))

    def chips(i):
        cs = pl.ds(*SPANS[i])
        return remote(R_YC + i, yc.at[:, cs], yo.at[:, cs], (tile, across))

    c_yb = [ends(i) for i in range(3)]
    c_yc = [chips(i) for i in range(3)]

    for g in range(2, 6):
        solve(g)
    c_yb[0].start()

    c_cof.wait_recv()
    upper = core == 0

    def pick(i, j):
        return jnp.where(upper, cfo[i], cfi[i]), jnp.where(upper, cfi[j], cfo[j])

    g_bu, g_bl = pick(1, 1)
    g_tu, g_tl = pick(0, 0)
    h_tu, h_tl = pick(2, 2)
    h_bu, h_bl = pick(3, 3)
    dd = 1.0 / (1.0 - g_tl * h_bu)
    mine = jnp.where(chip == 0, h_bl + g_bl * h_bu * dd * h_tl, g_tu + h_tu * dd * g_tl * g_bu)
    cho[...] = mine
    dq[0] = dd
    dq[1] = dd * (g_tl * g_bu + h_tl)
    dq[2] = g_tl
    dq[3] = h_bu
    dq[4] = g_bu
    dq[5] = g_bl
    dq[6] = h_tu
    c_chp = remote(R_CHP, cho, chi, (tile, across))
    c_chp.start()

    def merge(g):
        cs = pl.ds(g * GRP, GRP)
        yt_u = jnp.where(upper, yb[0, :, cs], yp[0, :, cs])
        yb_u = jnp.where(upper, yb[1, :, cs], yp[1, :, cs])
        yt_l = jnp.where(upper, yp[0, :, cs], yb[0, :, cs])
        yb_l = jnp.where(upper, yp[1, :, cs], yb[1, :, cs])
        t0 = bc(dq, 0, g) * (yt_l + bc(dq, 2, g) * yb_u)
        y0 = yb_l + bc(dq, 5, g) * (yb_u + bc(dq, 3, g) * t0)
        y1 = yt_u + bc(dq, 6, g) * t0
        yc[:, cs] = jnp.where(chip == 0, y0, y1)
        xe[0, :, cs] = t0
        xe[1, :, cs] = yb_u

    def finish(g):
        cs = pl.ds(g * GRP, GRP)
        one = pl.ds(g, 1)
        cm = cho[one, :]
        co = chi[one, :]
        scale = jnp.broadcast_to(1.0 / (1.0 - cm * co), (NTR, GRP))
        other = scale * (yo[:, cs] + jnp.broadcast_to(co, (NTR, GRP)) * yc[:, cs])
        t_l = xe[0, :, cs] + bc(dq, 1, g) * other
        b_u = xe[1, :, cs] + bc(dq, 3, g) * t_l + bc(dq, 4, g) * other
        xe[0, :, cs] = jnp.where(upper, other, b_u)
        xe[1, :, cs] = jnp.where(upper, t_l, other)

    out_g = []
    for g in range(8):
        hs = pl.ds(GRP * g, GRP)
        out_g.append(pltpu.make_async_copy(gf.at[:, g, :], g_out.at[:, hs], lsem.at[L_OUT + 1 + g]))
        out_g.append(pltpu.make_async_copy(hfo.at[:, g, :], h_out.at[:, hs], lsem.at[L_OUT + 9 + g]))
    for c in out_g:
        c.start()

    for j in range(4):
        own_part(j, 4 - j, 9)
        own_part(15 - j, 0, 5 + j)

    c_yb[0].wait_recv()

    for g in range(2, 6):
        merge(g)
    c_yc[0].start()

    for c in c_trc:
        c.wait_recv()
    for j in range(4):
        for b, lo, hi in ((j, 0, 4 - j), (15 - j, 5 + j, 9)):
            a = product(b, lo, hi, pl.ds(0, 256), False)
            mm[2 * b] = mm[2 * b] + 0.05 * a[:, :128]
            mm[2 * b + 1] = mm[2 * b + 1] + 0.05 * a[:, 128:]

    edges = (0, 1, 6, 7)
    for g in edges:
        solve(g)
    c_yb[1].start()
    c_yb[2].start()
    out_y = [
        pltpu.make_async_copy(mm.at[b], y_out.at[:, pl.ds(128 * b, 128)], lsem.at[L_OUT + 19 + b]) for b in range(32)
    ]
    for c in out_y:
        c.start()
    c_yb[1].wait_recv()
    c_yb[2].wait_recv()

    for g in edges:
        merge(g)
    c_yc[1].start()
    c_yc[2].start()

    for c in c_hal:
        c.wait_recv()
    for d in range(2):
        for i in range(2):
            cs = pl.ds(GRP * i, GRP)
            part = jnp.dot(tri[:LEV], vh[d, :, cs], preferred_element_type=F32)
            put_extra(
                pl.ds(d * (HALO + COLS) + GRP * i, GRP),
                blh[d, pl.ds(0, 1), cs] + part / LEVELS,
                blh[d, pl.ds(1, 1), cs],
            )
    for j in range(4):
        for b, lo, hi in ((j, 0, 4 - j), (15 - j, 5 + j, 9)):
            a = product(b, lo, hi, pl.ds(256, 80), False)
            cs = pl.ds(b * BLK, BLK)
            fo[:, cs] = fo[:, cs] + (a[:32] + a[48:80]) + vn[:, cs] * (a[32:33] + a[33:34])
    out_fo = pltpu.make_async_copy(fo, fo_out, lsem.at[L_OUT + 17])
    out_fo.start()

    c_chp.wait_recv()
    for c in c_yc:
        c.wait_recv()

    for g in range(8):
        finish(g)
    out_e = pltpu.make_async_copy(xe, ends_out, lsem.at[L_OUT + 18])
    out_e.start()

    for c in c_sum + [c_kap, c_cof, c_chp] + c_trc + c_hal + c_yb + c_yc:
        c.wait_send()
    for c in [out_gh] + out_g + out_y + [out_fo, out_e]:
        c.wait()


def combine(y_ref, e_ref, g_ref, h_ref, gh_ref, fo_ref, gh_out, fo_out, x_out):
    g = g_ref[...]
    h = h_ref[...]
    for n in range(NTR):
        x_out[n] = y_ref[n] + g * e_ref[0, pl.ds(n, 1), :] + h * e_ref[1, pl.ds(n, 1), :]
    gh_out[...] = gh_ref[...]
    fo_out[...] = fo_ref[...]


def local(thermal, humid, mixing, tracers, terrain, stress, share, table):
    f32 = lambda *s: jax.ShapeDtypeStruct(s, F32)
    vm = lambda *s: pltpu.VMEM(s, F32)
    vb = lambda *s: pltpu.VMEM(s, BF)
    fold = vm(LEV, 8, GRP)
    nat = vm(LEV, COLS)
    anyspec = pl.BlockSpec(memory_space=pl.ANY)
    y, ends, g, h, gh, fo = pl.pallas_call(
        kernel,
        out_shape=(f32(NTR * LEV, COLS), f32(2, NTR, COLS), f32(LEV, COLS), f32(LEV, COLS), f32(LEV, COLS), f32(LEV, COLS)),
        in_specs=[anyspec] * 8,
        out_specs=(anyspec,) * 6,
        scratch_shapes=[
            vb(ROWS, EXT), vb(NBLK, 2, WIN, BLK), vm(32, 256, 128), nat, nat, nat, nat, nat, fold, fold, fold,
            fold, fold, fold, fold, fold, vm(4, 1, COLS), vm(8, GRP), vm(8, GRP),
            vb(LEV, COLS), vb(2, LEV, HALO), vm(2, COLS), vm(2, 2, HALO),
            vm(4, 8, GRP), vm(4, 8, GRP), vm(8, GRP), vm(8, GRP), vm(7, 8, GRP),
            vm(2, NTR, COLS), vm(2, NTR, COLS), vm(NTR, COLS), vm(NTR, COLS), vm(2, NTR, COLS),
            vm(1, COLS), vm(1, COLS), vm(6, COLS), pltpu.VMEM((6, COLS), jnp.int32),
            vm(6, COLS), vb(6, COLS), vb(6, COLS), vm(1, COLS),
            pltpu.SemaphoreType.DMA((N_REMOTE,)), pltpu.SemaphoreType.DMA((N_REMOTE,)),
            pltpu.SemaphoreType.DMA((N_LOCAL + N_OUT,)),
        ],
        compiler_params=pltpu.CompilerParams(collective_id=0, has_side_effects=True, vmem_limit_bytes=67000000),
        name="band",
    )(thermal, humid, mixing, tracers, terrain[None], stress[None], share, table)
    width = 1024
    full = lambda *lead: pl.BlockSpec(lead + (width,), lambda i: (0,) * len(lead) + (i,))
    gh2, fo2, x = pl.pallas_call(
        combine,
        grid=(COLS // width,),
        out_shape=(f32(LEV, COLS), f32(LEV, COLS), f32(NTR, LEV, COLS)),
        in_specs=[full(NTR, LEV), full(2, NTR), full(LEV), full(LEV), full(LEV), full(LEV)],
        out_specs=(full(LEV), full(LEV), full(NTR, LEV)),
        name="combine",
    )(y.reshape(NTR, LEV, COLS), ends, g, h, gh, fo)
    return gh2, fo2, x


def solution(mesh):
    return jax.shard_map(
        local,
        mesh=mesh,
        in_specs=(
            P("lev", "tile"), P("lev", "tile"), P("lev", "tile"), P(None, "lev", "tile"),
            P("tile"), P("tile"), P(None, "tile"), P(None, "tile"),
        ),
        out_specs=(P("lev", "tile"), P("lev", "tile"), P(None, "lev", "tile")),
        check_vma=False,
    )
```

time: 570 us -> 67.8 us (0.12)
  local copies, waits for them, and re-layouts: 145 us -> 0 us
  other arithmetic: 129 us -> 0 us
  blocking collectives: 110 us -> 0 us
  matrix products: 97 us -> 0 us
  Pallas kernels: 0 us -> 66.3 us
  waiting for transfers between devices: 50.2 us -> 0 us
  starting transfers between devices: 16.8 us -> 0 us
  between operations: 14.9 us -> 0.64 us
    all_to_all x2 -> x0, blocking collectives: 110 us -> none  [the longest x1 59.7 us: local(): lax.all_to_all(packed, 'lev', split_axis=2, concat_axis=1, tiled=True)]
    dot_general x17 -> x0, matrix products: 97 us -> none  [the longest x8 47.9 us: stencil_block(): jnp.dot(tracer_window, weighting, precision=lax.Precision.HIGHEST, prefer...]
    pallas_call x0 -> x2, Pallas kernels: none -> 66.3 us  [the longest x1 60.7 us: local(): pl.pallas_call(kernel, out_shape=(f32(NTR * LEV, COLS), f32(2, NTR, COLS)...]
    reduce_sum x9 -> x0, other arithmetic: 54.6 us -> none  [the longest x8 54.6 us: stencil_block(): weighting = jnp.sum(jnp.where(hits, local_shares[:, None, :], 0.0), axis=0)]
    unnamed x40 -> x0, local copies, waits for them, and re-layouts: 54.2 us -> none
    ppermute x4 -> x0, waiting for transfers between devices: 38.5 us -> none  [the longest x2 19.3 us: extended(): lax.ppermute(head, axis, [((i + 1) % count, i) for i in range(count)])]
    all_to_all x4 -> x0, local copies, waits for them, and re-layouts: 32.5 us -> none  [the longest x2 21.8 us: local(): lax.all_to_all(packed, 'lev', split_axis=2, concat_axis=1, tiled=True)]
    slice x48 -> x0, local copies, waits for them, and re-layouts: 30.1 us -> none  [the longest x18 12 us: shift_down(): return jnp.concatenate([filler_block, values[..., :-stride, :]], axis=-2)]
  transfers between devices with their start and end apart: 6 -> 0, of which waited for: 5 -> 0; matrix products, arithmetic and copies ran while one was open for 1% -> 0% of each run, Pallas kernels for 0% -> 0%
where the time goes in v1:
time: 67.8 us; the launch traced here: 66.9 us
  Pallas kernels  66.3 us (98%)
    pallas_call x1, Pallas kernels, local(): pl.pallas_call(kernel, out_shape=(f32(NTR * LEV, COLS), f32(2, NTR, COLS)...  60.7 us
    pallas_call x1, Pallas kernels, local(): pl.pallas_call(combine, grid=(COLS // width,), out_shape=(f32(LEV, COLS),...  5.57 us

profile of v1, /device:TPU:1, one launch (start us, length us, event | category | flops | bytes accessed | tf_op | source)
XLA Modules:
  0.0 66.9 jit_solution(14255742763939380489)
XLA Ops:
  0.6 60.7 %band.1 = (f32[256,4096]{1,0:T(8,128)}, f32[2,8,4096]{2,1,0:T(8,128)}, f32[32,4096]{1,0:T(8,128)}, f32[32,4096]{1,0:T(8,128)}, f32[32,4096]{1,0:T(8,128)}, /*index=5*/f32[32,4096]{1,0:T(8,128)}) custom-call(f32[32,4096]{1,0:T(8,128)} %th_ref.1, f32[32,4096]{1,0:T(8,128)} %hu_ref.1, f32[32,4096]{1,0:T(8,128)} %mx_ref.1, bf16[8,32,4096]{2,1,0:T(8,128)(2,1)} %tr_ref.1, ...), custom_call_target="tpu_custom_call" | custom-call | tf_op jit(solution)/shard_map/band/pallas_call | solution.py:468
  61.4 5.6 %combine.1 = (f32[32,4096]{1,0:T(8,128)}, f32[32,4096]{1,0:T(8,128)}, f32[8,32,4096]{2,1,0:T(8,128)}) custom-call(f32[8,32,4096]{2,1,0:T(8,128)} %bitcast.3, f32[2,8,4096]{2,1,0:T(8,128)} %get-tuple-element.10.e_ref, f32[32,4096]{1,0:T(8,128)} %get-tuple-element.11.g_ref, f32[32,4096]{1,0:T(8,128)} %get-tuple-element.12.h_ref, ...), custom_call_target="tpu_custom_call" | custom-call | tf_op jit(solution)/shard_map/combine/pallas_call | solution.py:489

commit v2 on v1

v2 whole, which is shorter than its diff:
```python
import jax
import jax.numpy as jnp
from jax import lax
from jax.experimental import pallas as pl
from jax.experimental.pallas import tpu as pltpu
from jax.sharding import PartitionSpec as P

BF = jnp.bfloat16
F32 = jnp.float32
MESH = pl.DeviceIdType.MESH
HALO = 1024
COLS = 4096
EXT = COLS + 2 * HALO
LEV = 32
NTR = 8
BLK = 256
WIN = BLK + 2 * HALO
NBLK = COLS // BLK
GRP = 512
ROWS = 336
TILES = 32
LEVELS = 128.0

R_SUM = 0
R_KAP = 3
R_TRC = 4
R_VIR = 12
R_BAS = 14
R_COF = 16
R_CHP = 17
R_YB = 18
R_YC = 23
N_REMOTE = 28

L_NAT = 0
L_FOLD = 2
L_TRC = 26
L_SMALL = 34
N_LOCAL = 38
L_OUT = 38
N_OUT = 24
PART = 3
SPANS = ((1024, 2048), (512, 512), (3072, 512), (0, 512), (3584, 512))


def kernel(
    th_ref, hu_ref, mx_ref, tr_ref, te_ref, lo_ref, sh_ref, ad_ref,
    y_out, ends_out, g_out, h_out, gh_out, fo_out,
    xa, xh, xg, w0, w1, wh, mm, yk, fo, gh, vn, tn, hn, tf, hf, sf,
    rf, pf, ef, gf, hfo, sums, kbot, ktop, vb, vh, bl, blh,
    cfo, cfi, cho, chi, dq, yb, yp, yc, yo, xe, ter, los, shr, adj, shm, shi, slo, tot,
    ssem, rsem, lsem,
):
    tile = lax.axis_index("tile")
    lev = lax.axis_index("lev")
    core = lev % 2
    chip = lev // 2
    partner = chip * 2 + 1 - core
    across = (lev + 2) % 4
    diagonal = (partner + 2) % 4
    above = (lev + 3) % 4
    nxt = ((tile + 1) % TILES, lev)
    prv = ((tile + TILES - 1) % TILES, lev)
    peers = ((tile, partner), (tile, across), (tile, diagonal))

    bar = pltpu.get_barrier_semaphore()
    for q in peers + (nxt, prv):
        pl.semaphore_signal(bar, inc=1, device_id=q, device_id_type=MESH)

    def remote(i, src, dst, to):
        return pltpu.make_async_remote_copy(
            src_ref=src, dst_ref=dst, send_sem=ssem.at[i], recv_sem=rsem.at[i],
            device_id=to, device_id_type=MESH)

    nat = [pltpu.make_async_copy(s, d, lsem.at[L_NAT + i]) for i, (s, d) in enumerate(((th_ref, tn), (hu_ref, hn)))]
    small = [
        pltpu.make_async_copy(s, d, lsem.at[L_SMALL + i])
        for i, (s, d) in enumerate(((te_ref, ter), (lo_ref, los), (sh_ref, shr), (ad_ref, adj)))
    ]
    fold = []
    for i, (s, d) in enumerate(((th_ref, tf), (hu_ref, hf), (mx_ref, sf))):
        for g in range(8):
            fold.append(
                pltpu.make_async_copy(s.at[:, pl.ds(GRP * g, GRP)], d.at[:, g, :], lsem.at[L_FOLD + 8 * i + g])
            )
    trc = [
        pltpu.make_async_copy(tr_ref.at[n], xa.at[pl.ds(LEV * n, LEV), pl.ds(HALO, COLS)], lsem.at[L_TRC + n])
        for n in range(NTR)
    ]
    for c in nat + fold + small + trc:
        c.start()
    xa[:, pl.ds(0, HALO)] = jnp.zeros((ROWS, HALO), BF)
    xa[:, pl.ds(HALO + COLS, HALO)] = jnp.zeros((ROWS, HALO), BF)

    row = lax.broadcasted_iota(jnp.int32, (48, LEV), 0)
    col = lax.broadcasted_iota(jnp.int32, (48, LEV), 1)
    tri = jnp.where(row >= LEV, 1.0, jnp.where(col > row, 1.0, jnp.where(col == row, 0.5, 0.0))).astype(BF)
    for c in nat:
        c.wait()

    def natural(i, _):
        cs = pl.ds(pl.multiple_of(i * GRP, GRP), GRP)
        v = tn[:, cs] * (1.0 + 0.608 * hn[:, cs])
        vn[:, cs] = v
        v1 = v.astype(BF)
        vb[:, cs] = v1
        rest = v - v1.astype(F32)
        v2 = rest.astype(BF)
        v3 = (rest - v2.astype(F32)).astype(BF)
        part = jnp.dot(tri, v1, preferred_element_type=F32)
        part = part + jnp.dot(tri, v2, preferred_element_type=F32)
        part = part + jnp.dot(tri, v3, preferred_element_type=F32)
        gh[:, cs] = part[:LEV]
        sums[0, :, cs] = part[LEV : LEV + 1]
        return 0

    lax.fori_loop(0, 8, natural, 0)
    for c in fold:
        c.wait()
    for k in range(LEV):
        kap = sf[k] * (tf[k] * (1.0 + 0.608 * hf[k]))
        if k == 0:
            kap = jnp.where(lev == 0, 0.0, kap)
            ktop[...] = kap
        sf[k] = kap

    def step(k, below, e, gg):
        a = sf[k]
        d = 1.0 + a + below
        if k:
            d = d - a * e
        r = 1.0 / d
        p = a * r
        e = below * r
        gg = p * gg if k else p
        rf[k] = r
        pf[k] = p
        ef[k] = e
        gf[k] = gg
        return r, p, e, gg

    e = None
    gg = None
    for k in range(LEV - 1):
        _, _, e, gg = step(k, sf[k + 1], e, gg)
    for c in small:
        c.wait()

    t = [adj[pl.ds(m, 1), :] for m in range(6)]
    s = [shr[pl.ds(m, 1), :] for m in range(6)]
    total = s[0]
    for m in range(1, 6):
        total = total + s[m]
    tot[...] = total
    for m in range(6):
        acc = s[m]
        for q in range(m):
            acc = acc + jnp.where(t[q] == t[m], s[q], 0.0)
        shm[pl.ds(m, 1), :] = acc
    merged = shm[...]
    high = merged.astype(BF)
    shi[...] = high
    slo[...] = (merged - high.astype(F32)).astype(BF)

    ids = lax.broadcasted_iota(jnp.int32, (BLK, BLK), 0).astype(F32).astype(BF)

    def tables(j):
        cs = pl.ds(pl.multiple_of(j * BLK, BLK), BLK)
        place = (adj[:, cs] - j * BLK).astype(F32)
        high = shi[:, cs]
        low = slo[:, cs]
        hs = [jnp.broadcast_to(high[m : m + 1], (BLK, BLK)) for m in range(6)]
        ls = [jnp.broadcast_to(low[m : m + 1], (BLK, BLK)) for m in range(6)]
        return place, hs, ls

    def chunk(tab, offset):
        place, hs, ls = tab
        u = jnp.clip(place - offset, -1.0, float(BLK)).astype(BF)
        hi = jnp.zeros((BLK, BLK), BF)
        lw = jnp.zeros((BLK, BLK), BF)
        for m in range(6):
            hit = jnp.broadcast_to(u[m : m + 1], (BLK, BLK)) == ids
            hi = jnp.where(hit, hs[m], hi)
            lw = jnp.where(hit, ls[m], lw)
        return hi, lw

    def build(tab, w, r):
        hi, lw = chunk(tab, float(BLK * r))
        w[0, pl.ds(BLK * r, BLK), :] = hi
        w[1, pl.ds(BLK * r, BLK), :] = lw

    first = tables(4)
    for r in range(9):
        build(first, w0, r)

    pl.semaphore_wait(bar, 5)
    c_sum = [remote(R_SUM + d, sums.at[0], sums.at[1 + d], peers[d]) for d in range(3)]
    c_kap = remote(R_KAP, ktop, kbot, (tile, above))
    for c in c_sum:
        c.start()
    c_kap.start()
    c_trc = {}
    for i in range(4):
        for d, q, to in ((0, 3 - i, nxt), (1, i, prv)):
            src = tr_ref.at[:, :, pl.ds((COLS - HALO if d == 0 else 0) + BLK * q, BLK)]
            c_trc[d, q] = remote(R_TRC + 4 * d + q, src, xh.at[d, :, :, pl.ds(BLK * q, BLK)], to)
            c_trc[d, q].start()

    c_kap.wait_recv()
    r, p, e, gg = step(LEV - 1, kbot[...], e, gg)
    hh = e
    hfo[LEV - 1] = hh
    cfo[1] = gg
    cfo[3] = hh
    for k in range(LEV - 2, -1, -1):
        e = ef[k]
        gg = gf[k] + e * gg
        hh = e * hh
        gf[k] = gg
        hfo[k] = hh
    cfo[0] = gg
    cfo[2] = hh
    c_cof = remote(R_COF, cfo, cfi, (tile, partner))
    c_cof.start()

    for c in c_sum:
        c.wait_recv()
    peer_levs = (partner, across, diagonal)

    def split(v):
        hi = v.astype(BF)
        return hi, (v - hi.astype(F32)).astype(BF)

    sub16 = lax.broadcasted_iota(jnp.int32, (16, GRP), 0)

    def put_extra(ref, r0, cs, height, stress):
        hi, low = split(height)
        ref[pl.ds(r0, LEV), cs] = hi
        ref[pl.ds(r0 + 48, LEV), cs] = low
        shi_, slo_ = split(stress)
        both = jnp.where(
            sub16 == 0,
            jnp.broadcast_to(shi_.astype(F32), (16, GRP)),
            jnp.where(sub16 == 1, jnp.broadcast_to(slo_.astype(F32), (16, GRP)), 0.0),
        )
        ref[pl.ds(r0 + 32, 16), cs] = both.astype(BF)

    def heights(i, _):
        cs = pl.ds(pl.multiple_of(i * GRP, GRP), GRP)
        below = jnp.zeros((1, GRP), F32)
        for d in range(3):
            below = below + jnp.where(peer_levs[d] > lev, sums[1 + d, :, cs], 0.0)
        base = ter[:, cs] + below / LEVELS
        stress = los[:, cs]
        bl[pl.ds(0, 1), cs] = base
        bl[pl.ds(1, 1), cs] = stress
        height = base + gh[:, cs] / LEVELS
        gh[:, cs] = height
        put_extra(xa, 256, pl.ds(pl.multiple_of(HALO + i * GRP, GRP), GRP), height, stress)
        return 0

    lax.fori_loop(0, 8, heights, 0)
    c_hal = []
    for d, (lo, to) in enumerate(((COLS - HALO, nxt), (0, prv))):
        c_hal.append(remote(R_VIR + d, vb.at[:, pl.ds(lo, HALO)], vh.at[d], to))
        c_hal.append(remote(R_BAS + d, bl.at[:, pl.ds(lo, HALO)], blh.at[d], to))
    for c in c_hal:
        c.start()
    out_gh = pltpu.make_async_copy(gh, gh_out, lsem.at[L_OUT])
    out_gh.start()

    def fused(j, w, todo, lo=0, hi=9):
        parts = [range(q, min(q + PART, hi)) for q in range(lo, hi, PART)]
        share_out = -(-len(todo) // len(parts))
        high = None
        low = None
        for i, part in enumerate(parts):
            for work in todo[share_out * i : share_out * (i + 1)]:
                work()
            at = BLK * part[0]
            n = BLK * len(part)
            xs = pl.ds(pl.multiple_of(BLK * j, BLK) + at, n)
            d = jnp.dot(xa[:, xs], w[0, pl.ds(at, n), :], preferred_element_type=F32)
            high = d if high is None else high + d
            d = jnp.dot(xa[pl.ds(0, 304), xs], w[1, pl.ds(at, n), :], preferred_element_type=F32)
            low = d if low is None else low + d
        cs = pl.ds(pl.multiple_of(j * BLK, BLK), BLK)
        es = pl.ds(pl.multiple_of(HALO + j * BLK, BLK), BLK)
        total = tot[:, cs]
        own = xa[pl.ds(0, 256), es].astype(F32)
        mixed = own * (1.0 - 0.05 * total) + 0.05 * (high[:256] + low[:256])
        mm[2 * j] = mixed[:, :128]
        mm[2 * j + 1] = mixed[:, 128:]
        ends = high[288:290] + low[288:290]
        stress = ends[0:1] + ends[1:2] - los[:, cs] * total
        height = high[256:288] + low[256:288] + high[304:336]
        fo[:, cs] = (height - gh[:, cs] * total) + vn[:, cs] * stress

    def halo_product(c0, n, x):
        ws = pl.ds(BLK * c0, BLK * n)
        return jnp.dot(x, wh[0, ws, :], preferred_element_type=F32) + jnp.dot(
            x, wh[1, ws, :], preferred_element_type=F32
        )

    halo_parts = {}
    at = 0
    for j in range(4):
        halo_parts[j] = (at, 4 - j, 0, BLK * j)
        at += 4 - j
    for j in range(4):
        halo_parts[12 + j] = (at, j + 1, 1, 0)
        at += j + 1

    def own_range(b):
        return (4 - b, 9) if b < 4 else (0, 20 - b)

    def jobs(b, w, skip_own=False):
        tab = tables(b)
        lo, hi = own_range(b)
        c0 = halo_parts[b][0]

        def own(r):
            return lambda: build(tab, w, r)

        def far(i, r):
            def go():
                up, down = chunk(tab, float(BLK * r))
                ws = pl.ds(BLK * (c0 + i), BLK)
                wh[0, ws, :] = up
                wh[1, ws, :] = down

            return go

        beyond = [r for r in range(9) if not lo <= r < hi]
        out = [far(i, r) for i, r in enumerate(beyond)]
        return out if skip_own else [own(r) for r in range(lo, hi)] + out

    for c in trc:
        c.wait()

    def pair(i, _):
        j = 4 + 2 * i
        tab1 = tables(j + 1)
        fused(j, w0, [lambda r=r: build(tab1, w1, r) for r in range(9)])
        tab2 = tables(j + 2)
        fused(j + 1, w1, [lambda r=r: build(tab2, w0, r) for r in range(9)])
        return 0

    lax.fori_loop(0, 4, pair, 0)
    order = (12, 13, 14, 15, 3, 2, 1, 0)
    for i, b in enumerate(order):
        slot, other = (w0, w1) if i % 2 == 0 else (w1, w0)
        todo = jobs(order[i + 1], other) if i < 7 else []
        if i == 0:
            todo = todo + jobs(b, None, True)
        fused(b, slot, todo, *own_range(b))

    def bc(ref, k, g):
        return jnp.broadcast_to(ref[k, pl.ds(g, 1), :], (NTR, GRP))

    def solve(pair_of):
        chains = [(gi, q) for gi in pair_of for q in range(4)]

        def lane(ref, k, c):
            return jnp.broadcast_to(ref[k, pl.ds(c[0], 1), pl.ds(128 * c[1], 128)], (NTR, 128))

        f = [None] * 8
        for k in range(LEV):
            for i, c in enumerate(chains):
                b = 4 * c[0] + c[1]
                v = mm[b, pl.ds(k, NTR, stride=LEV), :] * lane(rf, k, c)
                f[i] = v + lane(pf, k, c) * f[i] if k else v
                yk[b, k] = f[i]
        for i, c in enumerate(chains):
            yb[1, :, pl.ds(c[0] * GRP + 128 * c[1], 128)] = f[i]
        for k in range(LEV - 2, -1, -1):
            for i, c in enumerate(chains):
                b = 4 * c[0] + c[1]
                f[i] = yk[b, k] + lane(ef, k, c) * f[i]
                yk[b, k] = f[i]
        for i, c in enumerate(chains):
            yb[0, :, pl.ds(c[0] * GRP + 128 * c[1], 128)] = f[i]

    def ends(i):
        cs = pl.ds(*SPANS[i])
        return remote(R_YB + i, yb.at[:, :, cs], yp.at[:, :, cs], (tile, partner))

    def chips(i):
        cs = pl.ds(*SPANS[i])
        return remote(R_YC + i, yc.at[:, cs], yo.at[:, cs], (tile, across))

    c_yb = [ends(i) for i in range(5)]
    c_yc = [chips(i) for i in range(5)]

    solve((2, 3))
    solve((4, 5))
    c_yb[0].start()
    runs = ((8, 16), (4, 4), (24, 4), (0, 4), (28, 4))

    def send_y(i):
        first, count = runs[i]

        def one(q, _):
            b = first + q
            ls = pl.ds(pl.multiple_of(b * 128, 128), 128)
            for n in range(NTR):
                pltpu.make_async_copy(yk.at[b, :, n, :], y_out.at[n, :, ls], lsem.at[L_OUT + 19 + i]).start()
            return 0

        lax.fori_loop(0, count, one, 0)

    def wait_y(i):
        first, count = runs[i]
        part = y_out.at[:, :, pl.ds(128 * first, 128 * count)]
        pltpu.make_async_copy(part, part, lsem.at[L_OUT + 19 + i]).wait()

    send_y(0)

    c_cof.wait_recv()
    upper = core == 0

    def pick(i, j):
        return jnp.where(upper, cfo[i], cfi[i]), jnp.where(upper, cfi[j], cfo[j])

    g_bu, g_bl = pick(1, 1)
    g_tu, g_tl = pick(0, 0)
    h_tu, h_tl = pick(2, 2)
    h_bu, h_bl = pick(3, 3)
    dd = 1.0 / (1.0 - g_tl * h_bu)
    mine = jnp.where(chip == 0, h_bl + g_bl * h_bu * dd * h_tl, g_tu + h_tu * dd * g_tl * g_bu)
    cho[...] = mine
    dq[0] = dd
    dq[1] = dd * (g_tl * g_bu + h_tl)
    dq[2] = g_tl
    dq[3] = h_bu
    dq[4] = g_bu
    dq[5] = g_bl
    dq[6] = h_tu
    c_chp = remote(R_CHP, cho, chi, (tile, across))
    c_chp.start()

    def merge(g):
        cs = pl.ds(g * GRP, GRP)
        yt_u = jnp.where(upper, yb[0, :, cs], yp[0, :, cs])
        yb_u = jnp.where(upper, yb[1, :, cs], yp[1, :, cs])
        yt_l = jnp.where(upper, yp[0, :, cs], yb[0, :, cs])
        yb_l = jnp.where(upper, yp[1, :, cs], yb[1, :, cs])
        t0 = bc(dq, 0, g) * (yt_l + bc(dq, 2, g) * yb_u)
        y0 = yb_l + bc(dq, 5, g) * (yb_u + bc(dq, 3, g) * t0)
        y1 = yt_u + bc(dq, 6, g) * t0
        yc[:, cs] = jnp.where(chip == 0, y0, y1)
        xe[0, :, cs] = t0
        xe[1, :, cs] = yb_u

    def finish(g):
        cs = pl.ds(g * GRP, GRP)
        one = pl.ds(g, 1)
        cm = cho[one, :]
        co = chi[one, :]
        scale = jnp.broadcast_to(1.0 / (1.0 - cm * co), (NTR, GRP))
        other = scale * (yo[:, cs] + jnp.broadcast_to(co, (NTR, GRP)) * yc[:, cs])
        t_l = xe[0, :, cs] + bc(dq, 1, g) * other
        b_u = xe[1, :, cs] + bc(dq, 3, g) * t_l + bc(dq, 4, g) * other
        xe[0, :, cs] = jnp.where(upper, other, b_u)
        xe[1, :, cs] = jnp.where(upper, t_l, other)

    out_g = []
    for g in range(8):
        hs = pl.ds(GRP * g, GRP)
        out_g.append(pltpu.make_async_copy(gf.at[:, g, :], g_out.at[:, hs], lsem.at[L_OUT + 1 + g]))
        out_g.append(pltpu.make_async_copy(hfo.at[:, g, :], h_out.at[:, hs], lsem.at[L_OUT + 9 + g]))
    for c in out_g:
        c.start()

    c_yb[0].wait_recv()

    for g in range(2, 6):
        merge(g)
    c_yc[0].start()

    stages = (
        (((0, 3), (1, 0), (0, 2), (1, 1)), (3, 12, 2, 13), (1, 6), (1, 2)),
        (((0, 1), (1, 2), (0, 0), (1, 3)), (1, 14, 0, 15), (0, 7), (3, 4)),
    )

    def join(groups, ids):
        for i in ids:
            c_yb[i].wait_recv()
        for g in groups:
            merge(g)
        for i in ids:
            c_yc[i].start()

    for chunks, blocks, groups, span_ids in stages:
        for key in chunks:
            c_trc[key].wait_recv()
        for b in blocks:
            c0, n, d, x0 = halo_parts[b]
            a = halo_product(c0, n, xh[d, :, :, pl.ds(x0, BLK * n)].reshape(256, BLK * n))
            mm[2 * b] = mm[2 * b] + 0.05 * a[:, :128]
            mm[2 * b + 1] = mm[2 * b + 1] + 0.05 * a[:, 128:]
        solve(groups)
        for i in span_ids:
            c_yb[i].start()
        for i in span_ids:
            send_y(i)
    join(*stages[0][2:])

    for c in c_hal:
        c.wait_recv()
    for d in range(2):
        for i in range(2):
            cs = pl.ds(GRP * i, GRP)
            part = jnp.dot(tri[:LEV], vh[d, :, cs], preferred_element_type=F32)
            put_extra(xg.at[d], 0, cs, blh[d, pl.ds(0, 1), cs] + part / LEVELS, blh[d, pl.ds(1, 1), cs])
    join(*stages[1][2:])
    for b, (c0, n, d, x0) in halo_parts.items():
        a = halo_product(c0, n, xg[d, :, pl.ds(x0, BLK * n)])
        cs = pl.ds(b * BLK, BLK)
        fo[:, cs] = fo[:, cs] + (a[:32] + a[48:80]) + vn[:, cs] * (a[32:33] + a[33:34])
    out_fo = pltpu.make_async_copy(fo, fo_out, lsem.at[L_OUT + 17])
    out_fo.start()

    c_chp.wait_recv()
    for c in c_yc:
        c.wait_recv()

    for g in range(8):
        finish(g)
    out_e = pltpu.make_async_copy(xe, ends_out, lsem.at[L_OUT + 18])
    out_e.start()

    for c in c_sum + [c_kap, c_cof, c_chp] + list(c_trc.values()) + c_hal + c_yb + c_yc:
        c.wait_send()
    for c in [out_gh] + out_g + [out_fo, out_e]:
        c.wait()
    for i in range(5):
        wait_y(i)


def combine(y_ref, e_ref, g_ref, h_ref, gh_ref, fo_ref, gh_out, fo_out, x_out):
    g = g_ref[...]
    h = h_ref[...]
    for n in range(NTR):
        x_out[n] = y_ref[n] + g * e_ref[0, pl.ds(n, 1), :] + h * e_ref[1, pl.ds(n, 1), :]
    gh_out[...] = gh_ref[...]
    fo_out[...] = fo_ref[...]


def local(thermal, humid, mixing, tracers, terrain, stress, share, table):
    f32 = lambda *s: jax.ShapeDtypeStruct(s, F32)
    vm = lambda *s: pltpu.VMEM(s, F32)
    vb = lambda *s: pltpu.VMEM(s, BF)
    fold = vm(LEV, 8, GRP)
    nat = vm(LEV, COLS)
    anyspec = pl.BlockSpec(memory_space=pl.ANY)
    y, ends, g, h, gh, fo = pl.pallas_call(
        kernel,
        out_shape=(f32(NTR, LEV, COLS), f32(2, NTR, COLS), f32(LEV, COLS), f32(LEV, COLS), f32(LEV, COLS), f32(LEV, COLS)),
        in_specs=[anyspec] * 8,
        out_specs=(anyspec,) * 6,
        scratch_shapes=[
            vb(ROWS, EXT), vb(2, NTR, LEV, HALO), vb(2, 80, HALO), vb(2, WIN, BLK), vb(2, WIN, BLK), vb(2, 20 * BLK, BLK),
            vm(32, 256, 128), vm(32, LEV, NTR, 128), nat, nat, nat, nat, nat, fold, fold, fold,
            fold, fold, fold, fold, fold, vm(4, 1, COLS), vm(8, GRP), vm(8, GRP),
            vb(LEV, COLS), vb(2, LEV, HALO), vm(2, COLS), vm(2, 2, HALO),
            vm(4, 8, GRP), vm(4, 8, GRP), vm(8, GRP), vm(8, GRP), vm(7, 8, GRP),
            vm(2, NTR, COLS), vm(2, NTR, COLS), vm(NTR, COLS), vm(NTR, COLS), vm(2, NTR, COLS),
            vm(1, COLS), vm(1, COLS), vm(6, COLS), pltpu.VMEM((6, COLS), jnp.int32),
            vm(6, COLS), vb(6, COLS), vb(6, COLS), vm(1, COLS),
            pltpu.SemaphoreType.DMA((N_REMOTE,)), pltpu.SemaphoreType.DMA((N_REMOTE,)),
            pltpu.SemaphoreType.DMA((N_LOCAL + N_OUT,)),
        ],
        compiler_params=pltpu.CompilerParams(collective_id=0, has_side_effects=True, vmem_limit_bytes=67000000),
        name="band",
    )(thermal, humid, mixing, tracers, terrain[None], stress[None], share, table)
    width = 1024
    full = lambda *lead: pl.BlockSpec(lead + (width,), lambda i: (0,) * len(lead) + (i,))
    gh2, fo2, x = pl.pallas_call(
        combine,
        grid=(COLS // width,),
        out_shape=(f32(LEV, COLS), f32(LEV, COLS), f32(NTR, LEV, COLS)),
        in_specs=[full(NTR, LEV), full(2, NTR), full(LEV), full(LEV), full(LEV), full(LEV)],
        out_specs=(full(LEV), full(LEV), full(NTR, LEV)),
        name="combine",
    )(y, ends, g, h, gh, fo)
    return gh2, fo2, x


def solution(mesh):
    return jax.shard_map(
        local,
        mesh=mesh,
        in_specs=(
            P("lev", "tile"), P("lev", "tile"), P("lev", "tile"), P(None, "lev", "tile"),
            P("tile"), P("tile"), P(None, "tile"), P(None, "tile"),
        ),
        out_specs=(P("lev", "tile"), P("lev", "tile"), P(None, "lev", "tile")),
        check_vma=False,
    )
```

time: 67.8 us -> 53.2 us (0.78)
  Pallas kernels: 66.3 us -> 52.3 us
    pallas_call x1, Pallas kernels: 60.7 us -> 46.8 us  [local(): pl.pallas_call(kernel, out_shape=(f32(NTR, LEV, COLS), f32(2, NTR, COLS),...]
where the time goes in v2:
time: 53.2 us; the launch traced here: 53 us
  Pallas kernels  52.3 us (98%)
  between operations  0.64 us (1%)
    pallas_call x1, Pallas kernels, local(): pl.pallas_call(kernel, out_shape=(f32(NTR, LEV, COLS), f32(2, NTR, COLS),...  46.8 us
    pallas_call x1, Pallas kernels, local(): pl.pallas_call(combine, grid=(COLS // width,), out_shape=(f32(LEV, COLS),...  5.57 us

profile of v2, /device:TPU:1, one launch (start us, length us, event | category | flops | bytes accessed | tf_op | source)
XLA Modules:
  0.0 53.0 jit_solution(7793247225837734225)
XLA Ops:
  0.6 46.8 %band.1 = (f32[8,32,4096]{2,1,0:T(8,128)}, f32[2,8,4096]{2,1,0:T(8,128)}, f32[32,4096]{1,0:T(8,128)}, f32[32,4096]{1,0:T(8,128)}, f32[32,4096]{1,0:T(8,128)}, /*index=5*/f32[32,4096]{1,0:T(8,128)}) custom-call(f32[32,4096]{1,0:T(8,128)} %th_ref.1, f32[32,4096]{1,0:T(8,128)} %hu_ref.1, f32[32,4096]{1,0:T(8,128)} %mx_ref.1, bf16[8,32,4096]{2,1,0:T(8,128)(2,1)} %tr_ref.1, ...), custom_call_target="tpu_custom_call" | custom-call | tf_op jit(solution)/shard_map/band/pallas_call | solution.py:557
  47.4 5.6 %combine.1 = (f32[32,4096]{1,0:T(8,128)}, f32[32,4096]{1,0:T(8,128)}, f32[8,32,4096]{2,1,0:T(8,128)}) custom-call(f32[8,32,4096]{2,1,0:T(8,128)} %get-tuple-element.9.y_ref, f32[2,8,4096]{2,1,0:T(8,128)} %get-tuple-element.10.e_ref, f32[32,4096]{1,0:T(8,128)} %get-tuple-element.11.g_ref, f32[32,4096]{1,0:T(8,128)} %get-tuple-element.12.h_ref, ...), custom_call_target="tpu_custom_call" | custom-call | tf_op jit(solution)/shard_map/combine/pallas_call | solution.py:579

commit v3 on v2

--- a/solution.py
+++ b/solution.py
@@ -39,7 +39,7 @@
 N_LOCAL = 38
 L_OUT = 38
 N_OUT = 24
-PART = 3
+PART = 1
 SPANS = ((1024, 2048), (512, 512), (3072, 512), (0, 512), (3584, 512))
 
 
@@ -506,6 +506,8 @@
             send_y(i)
     join(*stages[0][2:])
 
+    join(*stages[1][2:])
+
     for c in c_hal:
         c.wait_recv()
     for d in range(2):
@@ -513,7 +515,6 @@
             cs = pl.ds(GRP * i, GRP)
             part = jnp.dot(tri[:LEV], vh[d, :, cs], preferred_element_type=F32)
             put_extra(xg.at[d], 0, cs, blh[d, pl.ds(0, 1), cs] + part / LEVELS, blh[d, pl.ds(1, 1), cs])
-    join(*stages[1][2:])
     for b, (c0, n, d, x0) in halo_parts.items():
         a = halo_product(c0, n, xg[d, :, pl.ds(x0, BLK * n)])
         cs = pl.ds(b * BLK, BLK)
@@ -557,7 +558,7 @@
     y, ends, g, h, gh, fo = pl.pallas_call(
         kernel,
         out_shape=(f32(NTR, LEV, COLS), f32(2, NTR, COLS), f32(LEV, COLS), f32(LEV, COLS), f32(LEV, COLS), f32(LEV, COLS)),
-        in_specs=[anyspec] * 8,
+        in_specs=[pl.BlockSpec(memory_space=pltpu.HBM)] * 8,
         out_specs=(anyspec,) * 6,
         scratch_shapes=[
             vb(ROWS, EXT), vb(2, NTR, LEV, HALO), vb(2, 80, HALO), vb(2, WIN, BLK), vb(2, WIN, BLK), vb(2, 20 * BLK, BLK),
@@ -571,9 +572,9 @@
             pltpu.SemaphoreType.DMA((N_REMOTE,)), pltpu.SemaphoreType.DMA((N_REMOTE,)),
             pltpu.SemaphoreType.DMA((N_LOCAL + N_OUT,)),
         ],
-        compiler_params=pltpu.CompilerParams(collective_id=0, has_side_effects=True, vmem_limit_bytes=67000000),
+        compiler_params=pltpu.CompilerParams(collective_id=0, has_side_effects=True, vmem_limit_bytes=39 << 20),
         name="band",
-    )(thermal, humid, mixing, tracers, terrain[None], stress[None], share, table)
+    )(*[pltpu.with_memory_space_constraint(v, pltpu.HBM) for v in (thermal, humid, mixing, tracers, terrain[None], stress[None], share, table)])
     width = 1024
     full = lambda *lead: pl.BlockSpec(lead + (width,), lambda i: (0,) * len(lead) + (i,))
     gh2, fo2, x = pl.pallas_call(
@@ -582,6 +583,7 @@
         out_shape=(f32(LEV, COLS), f32(LEV, COLS), f32(NTR, LEV, COLS)),
         in_specs=[full(NTR, LEV), full(2, NTR), full(LEV), full(LEV), full(LEV), full(LEV)],
         out_specs=(full(LEV), full(LEV), full(NTR, LEV)),
+        compiler_params=pltpu.CompilerParams(vmem_limit_bytes=14 << 20),
         name="combine",
     )(y, ends, g, h, gh, fo)
     return gh2, fo2, x

time: 53.2 us -> 52.1 us (0.979)
  Pallas kernels: 52.3 us -> 51.4 us
    pallas_call x1, Pallas kernels: 5.57 us -> 3.22 us  [local(): pl.pallas_call(combine, grid=(COLS // width,), out_shape=(f32(LEV, COLS),...]
    pallas_call x1, Pallas kernels: 46.8 us -> 48.1 us  [local(): pl.pallas_call(kernel, out_shape=(f32(NTR, LEV, COLS), f32(2, NTR, COLS),...]
where the time goes in v3:
time: 52.1 us; the launch traced here: 52 us
  Pallas kernels  51.4 us (99%)
  between operations  0.64 us (1%)
    pallas_call x1, Pallas kernels, local(): pl.pallas_call(kernel, out_shape=(f32(NTR, LEV, COLS), f32(2, NTR, COLS),...  48.1 us
    pallas_call x1, Pallas kernels, local(): pl.pallas_call(combine, grid=(COLS // width,), out_shape=(f32(LEV, COLS),...  3.22 us

profile of v3, /device:TPU:1, one launch (start us, length us, event | category | flops | bytes accessed | tf_op | source)
XLA Modules:
  0.0 52.0 jit_solution(2005536036904807976)
XLA Ops:
  0.6 48.1 %band.1 = (f32[8,32,4096]{2,1,0:T(8,128)S(1)}, f32[2,8,4096]{2,1,0:T(8,128)S(1)}, f32[32,4096]{1,0:T(8,128)S(1)}, f32[32,4096]{1,0:T(8,128)S(1)}, f32[32,4096]{1,0:T(8,128)S(1)}, /*index=5*/f32[32,4096]{1,0:T(8,128)S(1)}) custom-call(f32[32,4096]{1,0:T(8,128)} %th_ref.1, f32[32,4096]{1,0:T(8,128)} %hu_ref.1, f32[32,4096]{1,0:T(8,128)} %mx_ref.1, ...), custom_call_target="tpu_custom_call" | custom-call | tf_op jit(solution)/shard_map/band/pallas_call | solution.py:558
  48.8 3.2 %combine.1 = (f32[32,4096]{1,0:T(8,128)}, f32[32,4096]{1,0:T(8,128)}, f32[8,32,4096]{2,1,0:T(8,128)}) custom-call(f32[8,32,4096]{2,1,0:T(8,128)S(1)} %get-tuple-element.9.y_ref, f32[2,8,4096]{2,1,0:T(8,128)S(1)} %get-tuple-element.10.e_ref, f32[32,4096]{1,0:T(8,128)S(1)} %get-tuple-element.11.g_ref, f32[32,4096]{1,0:T(8,128)S(1)} %get-tuple-element.12.h_ref, ...), custom_call_target="tpu_custom_call" | custom-call | tf_op jit(solution)/shard_map/combine/pallas_call | solution.py:580
